TPU v7x, 128 devices: a whole 4x4x4 slice. The times are simulated.
128 devices in a mesh: src: 32 (over y, x_hi, z), sta: 4 (over x_lo, core).
Axes of the slice: x: 4 (x_hi: 2, x_lo: 2; x = x_hi * 2 + x_lo), y: 4, z: 4, core: 2. Of those that a mesh axis runs over, the one named last changes fastest.
Arguments:
- trace: float32 [256, 8256], P('sta', 'src'), may hold values from -6 to 6
- quadrature: float32 [256, 8256], P('sta', 'src'), may hold values from -6 to 6
- gains: float32 [256], P('sta'), may hold values from 0.3 to 3
- lags: int32 [4096, 256], P('src', 'sta'), may hold values from 0 to 63
Outputs:
- beam_power: float32 [2, 4096], P(None, 'src')
All inputs are finite; a program needn't handle non-finite values.
Results may differ from a plain program's by a relative error of at most 0.0003.
Values may be sent and summed in bfloat16 or wider, within the bound.
No kernel may reach another device: no remote copies, remote signals or barrier semaphores. Data moves between devices by JAX's collectives and lax.ppermute only.
A program may use at most 256 MiB of HBM per device.

v0:
```python
import jax
import jax.numpy as jnp
from jax import lax
from jax.sharding import PartitionSpec as P

W = 4096
LAGS = 64
STEPS = 2


def on_device(trace, quadrature, gains, lags):
    energy = trace * trace + quadrature * quadrature
    row_totals = lax.psum(jnp.sum(energy, axis=1), "src")
    baseline = row_totals / (energy.shape[1] * lax.axis_size("src"))
    weighted = (gains[:, None] * (energy - baseline[:, None])).astype(jnp.bfloat16)
    envelope = lax.all_gather(weighted, "src", axis=1, tiled=True)
    cell_count, station_count = lags.shape
    offsets = jnp.arange(LAGS, dtype=jnp.int32)
    selector = (lags[:, None, :] == offsets[None, :, None]).astype(jnp.bfloat16)
    selector = selector.reshape(cell_count, LAGS * station_count)
    power_rows = []
    for step_index in range(STEPS):
        start = step_index * W
        stacked = jnp.concatenate(
            [envelope[:, start + lag_index : start + lag_index + W] for lag_index in range(LAGS)],
            axis=0,
        )
        partial_beam = jnp.dot(selector, stacked, preferred_element_type=jnp.float32)
        beam = lax.psum(partial_beam, "sta")
        power_rows.append(jnp.sum(beam * beam, axis=1))
    power = jnp.stack(power_rows)
    peak_power = lax.pmax(jnp.max(power, axis=1), "src")
    return power / peak_power[:, None]


def solution(mesh):
    return jax.shard_map(
        on_device,
        mesh=mesh,
        in_specs=(P("sta", "src"), P("sta", "src"), P("sta"), P("src", "sta")),
        out_specs=P(None, "src"),
        check_vma=False,
    )
```

profile of v0, /device:TPU:0, one launch (start us, length us, event | category | flops | bytes accessed | tf_op | source)
XLA Modules:
  0.0 483.9 jit_solution(4156925438073581276)
XLA Ops:
  7.6 97.9 %psum.21 = f32[64]{0:T(128)S(1)} all-reduce(f32[64]{0:T(128)S(1)} %fusion.1), channel_id=1, replica_groups=mesh['src'=32,'sta'=4] {'src'}, use_global_device_ids=true, to_apply=%region_1.0 | all-reduce | flops 64 | bytes 512 | tf_op jit(solution)/shard_map/psum | solution.py:13
  105.5 1.7 fusion
  107.3 1.5 bitcast_compare_fusion
  108.8 61.0 %all-gather.3.cloned.1.call-done = bf16[32,258,64]{1,2,0:T(8,128)(2,1)} async-done(((bf16[1,258,64]{1,2,0:T(8,128)(2,1)}), bf16[32,258,64]{1,2,0:T(8,128)(2,1)}) %all-gather.3.cloned.1.call-update) | async-done | bytes 1056784 | tf_op jit(solution)/shard_map/all_gather | solution.py:16
  169.9 2.3 copy.7
  172.2 1.9 reshape.8
  176.1 1.2 slice_dynamic-update-slice_fusion.125
  184.2 1.2 slice_dynamic-update-slice_fusion.118
  190.1 1.2 slice_dynamic-update-slice_fusion.113
  191.3 1.2 slice_dynamic-update-slice_fusion.112
  192.5 1.2 slice_dynamic-update-slice_fusion.111
  194.9 1.2 slice_dynamic-update-slice_fusion.109
  199.5 1.2 slice_dynamic-update-slice_fusion.105
  200.7 1.2 slice_dynamic-update-slice_fusion.104
  204.2 1.2 slice_dynamic-update-slice_fusion.101
  210.1 1.2 slice_dynamic-update-slice_fusion.96
  212.4 1.4 slice_dynamic-update-slice_fusion.94
  221.9 1.2 slice_dynamic-update-slice_fusion.86
  223.1 1.2 slice_dynamic-update-slice_fusion.85
  227.7 1.2 slice_dynamic-update-slice_fusion.81
  228.9 1.2 slice_dynamic-update-slice_fusion.80
  230.1 1.2 slice_dynamic-update-slice_fusion.79
  232.5 1.2 slice_dynamic-update-slice_fusion.77
  237.1 1.2 slice_dynamic-update-slice_fusion.73
  238.3 1.2 slice_dynamic-update-slice_fusion.72
  246.5 1.2 slice_dynamic-update-slice_fusion.65
  248.8 11.1 %copy-done = bf16[4096,4096]{1,0:T(8,128)(2,1)} copy-done((bf16[4096,4096]{1,0:T(8,128)(2,1)}, bf16[4096,4096]{1,0:T(8,128)(2,1)S(1)}, u32[]{:S(2)}) %copy-start) | copy-done | bytes 33554456
  259.9 14.4 %fusion.3 = f32[128,4096]{1,0:T(8,128)} fusion(pred[128,4096]{0,1:T(32,128)(4,1)S(1)} %bitcast_compare_fusion, bf16[4096,4096]{1,0:T(8,128)(2,1)} %copy-done), kind=kOutput, calls=%fused_computation.139 | convolution fusion | flops 4294967296 | bytes 36175872 | tf_op jit(solution)/shard_map/dot_general | solution.py:28
  274.3 14.3 %fusion.4 = f32[128,4096]{1,0:T(8,128)} fusion(pred[128,4096]{0,1:T(32,128)(4,1)S(1)} %bitcast_compare_fusion, bf16[4096,4096]{1,0:T(8,128)(2,1)} %get-tuple-element.8), kind=kOutput, calls=%fused_computation.140 | convolution fusion | flops 4294967296 | bytes 36175872 | tf_op jit(solution)/shard_map/dot_general | solution.py:28
  288.6 89.0 %all-reduce.3.cloned.1.call-done = (f32[128,4096]{1,0:T(8,128)}, f32[128,4096]{1,0:T(8,128)}) async-done(((f32[128,4096]{1,0:T(8,128)}, f32[128,4096]{1,0:T(8,128)}), (f32[128,4096]{1,0:T(8,128)}, f32[128,4096]{1,0:T(8,128)})) %all-reduce.3.cloned.1.call-update) | async-done | bytes 4194320 | tf_op jit(solution)/shard_map/psum | solution.py:29
  377.6 2.6 multiply_reduce_fusion
  380.3 96.1 %pmax.7 = f32[2]{0:T(128)S(1)} all-reduce(f32[2]{0:T(128)S(1)} %fusion.2), channel_id=1, replica_groups=mesh['src'=32,'sta'=4] {'src'}, use_global_device_ids=true, to_apply=%region_7.0 | all-reduce | flops 2 | bytes 16 | tf_op jit(solution)/shard_map/pmax | solution.py:32
  (55 shorter events, 52.7 us)
Async XLA Ops:
  6.5 163.3 %all-gather.3.cloned.1.call-start = ((), (), s32[]{:S(2)}) async-start(), calls=%async_computation | async-start | bytes 1622016 | tf_op jit(solution)/shard_map/all_gather | solution.py:16
  107.2 270.4 %all-reduce.3.cloned.1.call-start = ((), (), s32[]{:S(2)}) async-start(), calls=%async_computation.1 | async-start | bytes 8388608 | tf_op jit(solution)/shard_map/psum | solution.py:29
  248.8 11.1 %copy-start = (bf16[4096,4096]{1,0:T(8,128)(2,1)}, bf16[4096,4096]{1,0:T(8,128)(2,1)S(1)}, u32[]{:S(2)}) copy-start(bf16[4096,4096]{1,0:T(8,128)(2,1)S(1)} %get-tuple-element.7) | copy-start | bytes 100663296
Sparse Core Ops, SparseCore 0:
  107.3 62.4 all-gather.2
  288.8 88.8 all-reduce.2
where the time goes:
time: 484 us
  blocking collectives  194 us (40%)
  waiting for transfers between devices  150 us (31%)
  local copies, waits for them, and re-layouts  90.1 us (19%)
  matrix products  28.7 us (6%)
  between operations  13.5 us (3%)
  other arithmetic  7.54 us (2%)
    psum x1, blocking collectives, on_device(): row_totals = lax.psum(jnp.sum(energy, axis=1), 'src')  97.9 us
    pmax x1, blocking collectives, on_device(): peak_power = lax.pmax(jnp.max(power, axis=1), 'src')  96.1 us
    psum x1, waiting for transfers between devices, on_device(): beam = lax.psum(partial_beam, 'sta')  89 us
    unnamed x66, local copies, waits for them, and re-layouts  86.5 us
    all_gather x1, waiting for transfers between devices, on_device(): envelope = lax.all_gather(weighted, 'src', axis=1, tiled=True)  61 us
    dot_general x2, matrix products, on_device(): jnp.dot(selector, stacked, preferred_element_type=jnp.float32)  28.7 us
  transfers between devices with their start and end apart: 2, of which 2 were waited for; matrix products, arithmetic and copies ran while one was open for 0% of the time, Pallas kernels for 0%

commit v1 on v0

--- a/solution.py
+++ b/solution.py
@@ -13,7 +13,9 @@
     row_totals = lax.psum(jnp.sum(energy, axis=1), "src")
     baseline = row_totals / (energy.shape[1] * lax.axis_size("src"))
     weighted = (gains[:, None] * (energy - baseline[:, None])).astype(jnp.bfloat16)
-    envelope = lax.all_gather(weighted, "src", axis=1, tiled=True)
+    envelope = jnp.concatenate(
+        lax.all_to_all(jnp.stack([weighted] * lax.axis_size("src")), "src", 0, 0), axis=1
+    )
     cell_count, station_count = lags.shape
     offsets = jnp.arange(LAGS, dtype=jnp.int32)
     selector = (lags[:, None, :] == offsets[None, :, None]).astype(jnp.bfloat16)

time: 484 us -> 443 us (0.915)
  waiting for transfers between devices: 150 us -> 103 us
    all_gather x1 -> x0, waiting for transfers between devices: 61 us -> none  [on_device(): envelope = lax.all_gather(weighted, 'src', axis=1, tiled=True)]
    all_to_all x0 -> x1, waiting for transfers between devices: none -> 14.8 us  [on_device(): lax.all_to_all(jnp.stack([weighted] * lax.axis_size('src')), 'src', 0, 0)]
    reshape x0 -> x2, local copies, waits for them, and re-layouts: none -> 5.37 us  [on_device(): jnp.concatenate(lax.all_to_all(jnp.stack([weighted] * lax.axis_size('src'...]
    unnamed x66 -> x65, local copies, waits for them, and re-layouts: 86.5 us -> 84.9 us
where the time goes in v1:
time: 443 us
  blocking collectives  194 us (44%)
  waiting for transfers between devices  103 us (23%)
  local copies, waits for them, and re-layouts  92.9 us (21%)
  matrix products  28.7 us (6%)
  between operations  13.5 us (3%)
  other arithmetic  6.92 us (2%)
    psum x1, blocking collectives, on_device(): row_totals = lax.psum(jnp.sum(energy, axis=1), 'src')  97.9 us
    pmax x1, blocking collectives, on_device(): peak_power = lax.pmax(jnp.max(power, axis=1), 'src')  96.1 us
    psum x1, waiting for transfers between devices, on_device(): beam = lax.psum(partial_beam, 'sta')  88.1 us
    unnamed x65, local copies, waits for them, and re-layouts  84.9 us
    dot_general x2, matrix products, on_device(): jnp.dot(selector, stacked, preferred_element_type=jnp.float32)  28.7 us
    all_to_all x1, waiting for transfers between devices, on_device(): lax.all_to_all(jnp.stack([weighted] * lax.axis_size('src')), 'src', 0, 0)  14.8 us
  transfers between devices with their start and end apart: 2, of which 2 were waited for; matrix products, arithmetic and copies ran while one was open for 0% of the time, Pallas kernels for 0%

profile of v1, /device:TPU:0, one launch (start us, length us, event | category | flops | bytes accessed | tf_op | source)
XLA Modules:
  0.0 443.0 jit_solution(3545723839941779984)
XLA Ops:
  7.6 97.9 %psum.21 = f32[64]{0:T(128)S(1)} all-reduce(f32[64]{0:T(128)S(1)} %fusion), channel_id=1, replica_groups=mesh['src'=32,'sta'=4] {'src'}, use_global_device_ids=true, to_apply=%region_1.0 | all-reduce | flops 64 | bytes 512 | tf_op jit(solution)/shard_map/psum | solution.py:13
  106.6 1.4 stack.8
  108.0 4.0 all-to-all-start
  112.1 1.5 bitcast_compare_fusion
  113.6 14.8 %all-to-all-done = bf16[32,64,258]{2,1,0:T(8,128)(2,1)S(1)} async-done(((bf16[32,64,258]{2,1,0:T(8,128)(2,1)}), bf16[32,64,258]{2,1,0:T(8,128)(2,1)S(1)}, u32[]{:S(2)}, u32[]{:S(2)}) %all-to-all-start) | async-done | bytes 1056800 | tf_op jit(solution)/shard_map/all_to_all | solution.py:17
  128.4 2.1 copy.6
  130.5 3.3 reshape.16
  134.7 1.2 slice_dynamic-update-slice_fusion.126
  135.9 1.2 slice_dynamic-update-slice_fusion.125
  149.9 1.2 slice_dynamic-update-slice_fusion.113
  151.1 1.2 slice_dynamic-update-slice_fusion.112
  152.3 1.2 slice_dynamic-update-slice_fusion.111
  154.6 1.2 slice_dynamic-update-slice_fusion.109
  159.3 1.2 slice_dynamic-update-slice_fusion.105
  160.5 1.2 slice_dynamic-update-slice_fusion.104
  161.7 1.2 slice_dynamic-update-slice_fusion.103
  172.2 1.4 slice_dynamic-update-slice_fusion.94
  181.8 1.2 slice_dynamic-update-slice_fusion.86
  187.6 1.2 slice_dynamic-update-slice_fusion.81
  188.8 1.2 slice_dynamic-update-slice_fusion.80
  190.0 1.2 slice_dynamic-update-slice_fusion.79
  192.4 1.2 slice_dynamic-update-slice_fusion.77
  197.0 1.2 slice_dynamic-update-slice_fusion.73
  198.2 1.2 slice_dynamic-update-slice_fusion.72
  199.4 1.2 slice_dynamic-update-slice_fusion.71
  206.5 1.2 slice_dynamic-update-slice_fusion.65
  208.8 11.1 %copy-done = bf16[4096,4096]{1,0:T(8,128)(2,1)} copy-done((bf16[4096,4096]{1,0:T(8,128)(2,1)}, bf16[4096,4096]{1,0:T(8,128)(2,1)S(1)}, u32[]{:S(2)}) %copy-start) | copy-done | bytes 33554456
  219.8 14.4 %fusion.2 = f32[128,4096]{1,0:T(8,128)} fusion(pred[128,4096]{0,1:T(32,128)(4,1)S(1)} %bitcast_compare_fusion, bf16[4096,4096]{1,0:T(8,128)(2,1)} %copy-done), kind=kOutput, calls=%fused_computation.138 | convolution fusion | flops 4294967296 | bytes 36175872 | tf_op jit(solution)/shard_map/dot_general | solution.py:30
  234.2 14.3 %fusion.3 = f32[128,4096]{1,0:T(8,128)} fusion(pred[128,4096]{0,1:T(32,128)(4,1)S(1)} %bitcast_compare_fusion, bf16[4096,4096]{1,0:T(8,128)(2,1)} %get-tuple-element.8), kind=kOutput, calls=%fused_computation.139 | convolution fusion | flops 4294967296 | bytes 36175872 | tf_op jit(solution)/shard_map/dot_general | solution.py:30
  248.6 88.1 %all-reduce.3.cloned.1.call-done = (f32[128,4096]{1,0:T(8,128)}, f32[128,4096]{1,0:T(8,128)}) async-done(((f32[128,4096]{1,0:T(8,128)}, f32[128,4096]{1,0:T(8,128)}), (f32[128,4096]{1,0:T(8,128)}, f32[128,4096]{1,0:T(8,128)})) %all-reduce.3.cloned.1.call-update) | async-done | bytes 4194320 | tf_op jit(solution)/shard_map/psum | solution.py:31
  336.7 2.6 multiply_reduce_fusion
  339.4 96.1 %pmax.7 = f32[2]{0:T(128)S(1)} all-reduce(f32[2]{0:T(128)S(1)} %fusion.1), channel_id=1, replica_groups=mesh['src'=32,'sta'=4] {'src'}, use_global_device_ids=true, to_apply=%region_7.0 | all-reduce | flops 2 | bytes 16 | tf_op jit(solution)/shard_map/pmax | solution.py:34
  (55 shorter events, 55.1 us)
Async XLA Ops:
  108.0 20.4 %all-to-all-start = ((bf16[32,64,258]{2,1,0:T(8,128)(2,1)}), bf16[32,64,258]{2,1,0:T(8,128)(2,1)S(1)}, u32[]{:S(2)}, u32[]{:S(2)}) async-start(bf16[32,64,258]{2,1,0:T(8,128)(2,1)} %stack.8), calls=%async_computation | async-start | bytes 3145728 | tf_op jit(solution)/shard_map/all_to_all | solution.py:17
  112.0 224.7 %all-reduce.3.cloned.1.call-start = ((), (), s32[]{:S(2)}) async-start(), calls=%async_computation.1 | async-start | bytes 8388608 | tf_op jit(solution)/shard_map/psum | solution.py:31
  208.8 11.1 %copy-start = (bf16[4096,4096]{1,0:T(8,128)(2,1)}, bf16[4096,4096]{1,0:T(8,128)(2,1)S(1)}, u32[]{:S(2)}) copy-start(bf16[4096,4096]{1,0:T(8,128)(2,1)S(1)} %get-tuple-element.7) | copy-start | bytes 100663296
Sparse Core Ops, SparseCore 0:
  248.7 87.9 all-reduce.2
